TPU v7x, 32 devices: a whole 2x2x4 slice. The times are simulated.
32 devices in a mesh: gz: 2 (over core), gx: 4 (over z), gy: 4 (over y, x).
Axes of the slice: x: 2, y: 2, z: 4, core: 2. Of those that a mesh axis runs over, the one named last changes fastest.
Arguments:
- pair_repr: bfloat16 [8, 384, 384, 128], P('gz', 'gx', 'gy'), may hold values from -9 to 9
- seq_lengths: int32 [8], replicated, may hold values from 96 to 384
- weight_in: bfloat16 [128, 640], replicated, may hold values from -0.5 to 0.5
- weight_out: bfloat16 [128, 128], replicated, may hold values from -0.5 to 0.5
Outputs:
- updated: bfloat16 [8, 384, 384, 128], P('gz', 'gx', 'gy')
- magnitude: float32 [], replicated
All inputs are finite; a program needn't handle non-finite values.
Results may differ from a plain program's by a relative error of at most 0.0034.
Values may be sent and summed in bfloat16 or wider, within the bound.
A program may use at most 384 MiB of HBM per device.

v0:
```python
import jax
import jax.numpy as jnp
from jax import lax
from jax.sharding import PartitionSpec as P


def layer_norm(values):
    mean_value = jnp.mean(values, axis=-1, keepdims=True)
    centered = values - mean_value
    variance = jnp.mean(centered * centered, axis=-1, keepdims=True)
    return centered * lax.rsqrt(variance + 1e-05)


def per_device(pair_repr, seq_lengths, weight_in, weight_out):
    batch_dev, row_count, col_count, channels = pair_repr.shape
    hidden = weight_out.shape[0]
    row_first = lax.axis_index("gx") * row_count
    col_first = lax.axis_index("gy") * col_count
    my_lengths = lax.dynamic_slice_in_dim(seq_lengths, lax.axis_index("gz") * batch_dev, batch_dev)
    row_live = (
        (row_first + jnp.arange(row_count, dtype=jnp.int32))[None, :] < my_lengths[:, None]
    ).astype(jnp.float32)
    col_live = (
        (col_first + jnp.arange(col_count, dtype=jnp.int32))[None, :] < my_lengths[:, None]
    ).astype(jnp.float32)
    pair_mask = row_live[:, :, None, None] * col_live[:, None, :, None]
    normed = layer_norm(pair_repr.astype(jnp.float32)).astype(jnp.bfloat16)
    proj = jnp.dot(normed.reshape(-1, channels), weight_in, preferred_element_type=jnp.float32)
    proj = proj.reshape(batch_dev, row_count, col_count, 4 * hidden + channels)
    left_proj = (
        pair_mask * jax.nn.sigmoid(proj[..., hidden : 2 * hidden]) * proj[..., :hidden]
    ).astype(jnp.bfloat16)
    right_proj = (
        pair_mask
        * jax.nn.sigmoid(proj[..., 3 * hidden : 4 * hidden])
        * proj[..., 2 * hidden : 3 * hidden]
    ).astype(jnp.bfloat16)
    gate_values = jax.nn.sigmoid(proj[..., 4 * hidden :])
    left_rows = lax.all_gather(left_proj, "gy", axis=2, tiled=True)
    triangle = lax.psum_scatter(
        jnp.einsum("bkic,bkjc->ibjc", left_rows, right_proj, preferred_element_type=jnp.float32),
        "gx",
        scatter_dimension=0,
        tiled=True,
    ).transpose(1, 0, 2, 3)
    tri_normed = layer_norm(triangle).astype(jnp.bfloat16)
    projected = jnp.dot(
        tri_normed.reshape(-1, hidden), weight_out, preferred_element_type=jnp.float32
    )
    update = pair_mask * gate_values * projected.reshape(batch_dev, row_count, col_count, channels)
    updated = (pair_repr.astype(jnp.float32) + update).astype(jnp.bfloat16)
    mag_total = lax.psum(jnp.sum(jnp.abs(updated.astype(jnp.float32))), ("gz", "gx", "gy"))
    entry_count = (
        batch_dev
        * lax.axis_size("gz")
        * row_count
        * lax.axis_size("gx")
        * col_count
        * lax.axis_size("gy")
        * channels
    )
    magnitude = mag_total / float(entry_count)
    return (updated, magnitude)


def solution(mesh):
    return jax.shard_map(
        per_device,
        mesh=mesh,
        in_specs=(P("gz", "gx", "gy", None), P(), P(), P()),
        out_specs=(P("gz", "gx", "gy", None), P()),
        check_vma=False,
    )
```

profile of v0, /device:TPU:0, one launch (start us, length us, event | category | flops | bytes accessed | tf_op | source)
XLA Modules:
  0.0 1928.3 jit_solution(4665323842671105587)
XLA Ops:
  7.2 0.0 copy-start
  7.2 0.0 copy-start.4
  7.2 0.0 all-gather.2.cloned.1.call-start
  7.2 7.2 convert_reduce_fusion
  14.5 13.8 fusion.2
  28.3 0.0 copy-done.4
  28.3 0.1 dynamic_slice.3
  28.4 0.1 compare_convert_fusion.1
  28.4 0.1 broadcast_multiply_fusion.1
  28.6 0.0 copy-done
  28.6 35.3 %fusion.20 = f32[4,96,96,640]{3,2,1,0:T(8,128)} fusion(bf16[4,96,96,128]{3,2,1,0:T(8,128)(2,1)} %param.4, f32[4,96,96]{2,1,0:T(8,128)S(1)} %add_rsqrt_fusion, f32[4,96,96]{2,1,0:T(8,128)S(1)} %broadcast_multiply_fusion, bf16[128,640]{1,0:T(8,128)(2,1)S(1)} %copy-done), kind=kOutput, calls=%fused_computation.34 | convolution fusion | flops 6058672128 | bytes 104267776 | tf_op jit(solution)/shard_map/dot_general | solution.py:28
  63.9 32.3 %fusion.5 = (bf16[4,96,96,128]{3,2,1,0:T(8,128)(2,1)}, bf16[4,96,96,128]{3,2,1,0:T(8,128)(2,1)}) fusion(f32[4,96,96,640]{3,2,1,0:T(8,128)} %fusion.20, f32[4,96,96]{2,1,0:T(8,128)S(1)} %broadcast_multiply_fusion.1), kind=kLoop, calls=%fused_computation.10 | loop fusion | flops 56623104 | bytes 94519296 | tf_op jit(solution)/shard_map/convert_element_type | solution.py:32
  96.2 0.0 all-gather.2.cloned.1.call-update
  96.2 0.2 reduce-scatter.2.cloned.1.call-start
  96.5 17.9 copy.21
  114.4 317.6 %all-gather.2.cloned.1.call-done = bf16[4,96,384,128]{3,2,1,0:T(8,128)(2,1)} async-done(((bf16[4,96,96,128]{3,2,1,0:T(8,128)(2,1)}), bf16[4,96,384,128]{3,2,1,0:T(8,128)(2,1)}) %all-gather.2.cloned.1.call-update) | async-done | bytes 37748752 | tf_op jit(solution)/shard_map/all_gather | solution.py:39
  432.0 47.5 %copy.22 = bf16[4,96,384,128]{2,1,3,0:T(8,128)(2,1)} copy(bf16[4,96,384,128]{3,2,1,0:T(8,128)(2,1)} %all-gather.2.cloned.1.call-done) | data formatting | bytes 75497472 | tf_op jit(solution)/shard_map/all_gather | solution.py:39
  479.4 42.3 %convolution_bitcast_fusion = f32[384,4,96,128]{0,2,3,1:T(8,128)} fusion(bf16[4,96,96,128]{1,2,3,0:T(8,128)(2,1)} %copy.21, bf16[4,96,384,128]{2,1,3,0:T(8,128)(2,1)} %copy.22), kind=kOutput, calls=%fused_computation | convolution fusion | flops 3623878656 | bytes 122683392 | tf_op jit(solution)/shard_map/bkic,bkjc->ibjc/dot_general | solution.py:41
  521.7 74.3 %copy.23 = f32[384,4,96,128]{3,2,1,0:T(8,128)} copy(f32[384,4,96,128]{0,2,3,1:T(8,128)} %convolution_bitcast_fusion) | data formatting | bytes 150994944 | tf_op jit(solution)/shard_map/bkic,bkjc->ibjc/transpose | solution.py:41
  595.9 0.0 reduce-scatter.2.cloned.1.call-update
  596.0 0.0 copy-start.3
  596.0 1230.4 %reduce-scatter.2.cloned.1.call-done = f32[96,4,96,128]{3,2,1,0:T(8,128)} async-done(((f32[384,4,96,128]{3,2,1,0:T(8,128)}), f32[96,4,96,128]{3,2,1,0:T(8,128)}) %reduce-scatter.2.cloned.1.call-update) | async-done | bytes 18874384 | tf_op jit(solution)/shard_map/reduce_scatter | solution.py:40
  1826.3 0.0 slice-start
  1826.4 0.0 slice-start.1
  1826.4 0.0 copy-start.2
  1826.4 11.5 bitcast_reduce_fusion
  1837.9 0.1 copy.26
  1838.1 0.0 slice-start.2
  1838.1 15.2 multiply_reduce_fusion
  1853.3 0.1 copy.29
  1853.4 0.0 copy-done.3
  1853.4 0.0 slice-done
  1853.4 0.0 slice-done.1
  1853.4 0.0 copy-done.2
  1853.5 0.0 slice-done.2
  1853.5 0.0 copy-start.1
  1853.5 24.9 %abs_reduce_fusion = (f32[]{:T(128)}, bf16[4,96,96,128]{3,2,1,0:T(8,128)(2,1)}) fusion(bf16[128,128]{1,0:T(8,128)(2,1)S(1)} %copy-done.3, f32[4,96,96,640]{3,2,1,0:T(8,128)} %fusion.20, f32[4,96,96]{2,1,0:T(8,128)S(1)} %broadcast_multiply_fusion.1, bf16[4,96,96,128]{3,2,1,0:T(8,128)(2,1)S(1)} %bitcast.29, f32[96,4,96,128]{3,2,1,0:T(8,128)S(1)} %copy-done.2, ...), kind=kOutput, calls=%fused_computation.31 | convolution fusion | flops 1274019840 | bytes 57098244 | tf_op jit(solution)/shard_map/dot_general | solution.py:47
  1878.4 41.3 %psum.7 = f32[]{:T(128)} all-reduce(f32[]{:T(128)} %get-tuple-element.6), channel_id=1, replica_groups=mesh['gz'=2,'gx'=4,'gy'=4] {'gz','gx','gy'}, use_global_device_ids=true, to_apply=%region_6.0 | all-reduce | flops 1 | bytes 8 | tf_op jit(solution)/shard_map/psum | solution.py:52
  1920.4 0.0 copy-done.1
  (6 shorter events, 0.1 us)
Async XLA Ops:
  7.2 21.4 %copy-start = (bf16[128,640]{1,0:T(8,128)(2,1)S(1)}, bf16[128,640]{1,0:T(8,128)(2,1)}, u32[]{:S(2)}) copy-start(bf16[128,640]{1,0:T(8,128)(2,1)} %param.6) | copy-start | bytes 491524
  7.2 21.1 %copy-start.4 = (s32[8]{0:T(128)S(1)}, s32[8]{0:T(128)}, u32[]{:S(2)}) copy-start(s32[8]{0:T(128)} %param.5) | copy-start | bytes 100
  7.2 424.8 %all-gather.2.cloned.1.call-start = ((), (), s32[]{:S(2)}) async-start(), calls=%async_computation.1 | async-start | bytes 47185920 | tf_op jit(solution)/shard_map/all_gather | solution.py:39
  96.2 1730.1 %reduce-scatter.2.cloned.1.call-start = ((), (), s32[]{:S(2)}) async-start(), calls=%async_computation.2 | async-start | bytes 94371840 | tf_op jit(solution)/shard_map/reduce_scatter | solution.py:40
  596.0 1257.4 %copy-start.3 = (bf16[128,128]{1,0:T(8,128)(2,1)S(1)}, bf16[128,128]{1,0:T(8,128)(2,1)}, u32[]{:S(2)}) copy-start(bf16[128,128]{1,0:T(8,128)(2,1)} %param.7) | copy-start | bytes 98308
  1826.3 27.1 %slice-start = ((s8[9437184]{0:T(1024)(128)(4,1)}), s8[4194304]{0:T(1024)(128)(4,1)S(1)}, s32[]{:S(2)}) async-start(s8[9437184]{0:T(1024)(128)(4,1)} %bitcast.28), calls=%async_computation.3 | async-start | bytes 8388608
  1826.4 27.1 %slice-start.1 = ((s8[9437184]{0:T(1024)(128)(4,1)}), s8[1048576]{0:T(1024)(128)(4,1)S(1)}, s32[]{:S(2)}) async-start(s8[9437184]{0:T(1024)(128)(4,1)} %bitcast.28), calls=%async_computation.4 | async-start | bytes 2097152
  1826.4 27.1 %copy-start.2 = (f32[96,4,96,128]{3,2,1,0:T(8,128)S(1)}, f32[96,4,96,128]{3,2,1,0:T(8,128)}, u32[]{:S(2)}) copy-start(f32[96,4,96,128]{3,2,1,0:T(8,128)} %reduce-scatter.2.cloned.1.call-done) | copy-start | bytes 56623108
  1838.1 15.4 slice-start.2
  1853.5 66.9 %copy-start.1 = (bf16[128,640]{1,0:T(8,128)(2,1)S(1)}, bf16[128,640]{1,0:T(8,128)(2,1)}, u32[]{:S(2)}) copy-start(bf16[128,640]{1,0:T(8,128)(2,1)} %param.6) | copy-start | bytes 491524
Sparse Core Ops, SparseCore 0:
  96.4 335.5 all-gather.1
  596.1 1230.2 reduce-scatter.1
where the time goes:
time: 1930 us
  waiting for transfers between devices  1550 us (80%)
  local copies, waits for them, and re-layouts  140 us (7%)
  matrix products  102 us (5%)
  other arithmetic  80.2 us (4%)
  blocking collectives  41.3 us (2%)
    reduce_scatter x1, waiting for transfers between devices, per_device(): lax.psum_scatter(jnp.einsum('bkic,bkjc->ibjc', left_rows, right_proj, pre...  1230 us
    all_gather x1, waiting for transfers between devices, per_device(): left_rows = lax.all_gather(left_proj, 'gy', axis=2, tiled=True)  318 us
    transpose x1, local copies, waits for them, and re-layouts, per_device(): jnp.einsum('bkic,bkjc->ibjc', left_rows, right_proj, preferred_element_ty...  74.3 us
    all_gather x1, local copies, waits for them, and re-layouts, per_device(): left_rows = lax.all_gather(left_proj, 'gy', axis=2, tiled=True)  47.5 us
    dot_general x1, matrix products, per_device(): jnp.einsum('bkic,bkjc->ibjc', left_rows, right_proj, preferred_element_ty...  42.3 us
    psum x1, blocking collectives, per_device(): lax.psum(jnp.sum(jnp.abs(updated.astype(jnp.float32))), ('gz', 'gx', 'gy'))  41.3 us
  transfers between devices with their start and end apart: 2, of which 2 were waited for; matrix products, arithmetic and copies ran while one was open for 1% of the time, Pallas kernels for 0%

commit v1 on v0

v1 whole, which is shorter than its diff:
```python
import jax
import jax.numpy as jnp
from jax import lax
from jax.sharding import PartitionSpec as P


def layer_norm(values):
    mean_value = jnp.mean(values, axis=-1, keepdims=True)
    centered = values - mean_value
    variance = jnp.mean(centered * centered, axis=-1, keepdims=True)
    return centered * lax.rsqrt(variance + 1e-05)


def per_device(pair_repr, seq_lengths, weight_in, weight_out):
    batch_dev, row_count, col_count, channels = pair_repr.shape
    hidden = weight_out.shape[0]
    row_first = lax.axis_index("gx") * row_count
    col_first = lax.axis_index("gy") * col_count
    my_lengths = lax.dynamic_slice_in_dim(seq_lengths, lax.axis_index("gz") * batch_dev, batch_dev)
    row_at = row_first + jnp.arange(row_count, dtype=jnp.int32)
    col_at = col_first + jnp.arange(col_count, dtype=jnp.int32)

    def gated(normed, first, mask):
        part = weight_in[:, first : first + 2 * hidden]
        proj = jnp.einsum("ijc,cd->ijd", normed, part, preferred_element_type=jnp.float32)
        return (mask * jax.nn.sigmoid(proj[..., hidden:]) * proj[..., :hidden]).astype(
            jnp.bfloat16
        )

    masks, normed, gathered, shares = [], [], [], []
    for b in range(batch_dev):
        row_live = (row_at < my_lengths[b]).astype(jnp.float32)
        col_live = (col_at < my_lengths[b]).astype(jnp.float32)
        masks.append(row_live[:, None, None] * col_live[None, :, None])
        normed.append(layer_norm(pair_repr[b].astype(jnp.float32)).astype(jnp.bfloat16))
        left = gated(normed[b], 0, masks[b])
        gathered.append(lax.all_gather(left, "gy", axis=1, tiled=True))
    for b in range(batch_dev):
        right = gated(normed[b], 2 * hidden, masks[b])
        partial = jnp.einsum(
            "kic,kjc->ijc", gathered[b], right, preferred_element_type=jnp.float32
        ).astype(jnp.bfloat16)
        shares.append(lax.psum_scatter(partial, "gx", scatter_dimension=0, tiled=True))
    outs, total = [], jnp.float32(0)
    for b in range(batch_dev):
        gate_values = jax.nn.sigmoid(
            jnp.einsum(
                "ijc,cd->ijd", normed[b], weight_in[:, 4 * hidden :],
                preferred_element_type=jnp.float32,
            )
        )
        tri_normed = layer_norm(shares[b].astype(jnp.float32)).astype(jnp.bfloat16)
        projected = jnp.einsum(
            "ijc,cd->ijd", tri_normed, weight_out, preferred_element_type=jnp.float32
        )
        update = masks[b] * gate_values * projected
        one = (pair_repr[b].astype(jnp.float32) + update).astype(jnp.bfloat16)
        outs.append(one)
        total = total + jnp.sum(jnp.abs(one.astype(jnp.float32)))
    updated = jnp.stack(outs)
    mag_total = lax.psum(total, ("gz", "gx", "gy"))
    entry_count = (
        batch_dev
        * lax.axis_size("gz")
        * row_count
        * lax.axis_size("gx")
        * col_count
        * lax.axis_size("gy")
        * channels
    )
    magnitude = mag_total / float(entry_count)
    return (updated, magnitude)


def solution(mesh):
    return jax.shard_map(
        per_device,
        mesh=mesh,
        in_specs=(P("gz", "gx", "gy", None), P(), P(), P()),
        out_specs=(P("gz", "gx", "gy", None), P()),
        check_vma=False,
    )
```

time: 1930 us -> 1190 us (0.62)
  waiting for transfers between devices: 1550 us -> 772 us
  matrix products: 102 us -> 139 us
    reduce_scatter x1 -> x4, waiting for transfers between devices: 1230 us -> 563 us  [per_device(): lax.psum_scatter(partial, 'gx', scatter_dimension=0, tiled=True)]
    all_gather x1 -> x4, waiting for transfers between devices: 318 us -> 209 us  [per_device(): gathered.append(lax.all_gather(left, 'gy', axis=1, tiled=True))]
    transpose x1 -> x0, local copies, waits for them, and re-layouts: 74.3 us -> none  [per_device(): jnp.einsum('bkic,bkjc->ibjc', left_rows, right_proj, preferred_element_ty...]
    convert_element_type x1 -> x8, local copies, waits for them, and re-layouts: 17.9 us -> 72.3 us  [the longest x4 55.6 us: per_device(): partial = jnp.einsum('kic,kjc->ijc', gathered[b], right, preferred_elemen...]
    dot_general x3 -> x20, matrix products: 102 us -> 139 us  [the longest x8 51.6 us: gated(): jnp.einsum('ijc,cd->ijd', normed, part, preferred_element_type=jnp.float32)]
    all_gather x1 -> x4, local copies, waits for them, and re-layouts: 47.5 us -> 52.1 us  [per_device(): gathered.append(lax.all_gather(left, 'gy', axis=1, tiled=True))]
  transfers between devices with their start and end apart: 2 -> 8, of which waited for: 2 -> 8; matrix products, arithmetic and copies ran while one was open for 1% -> 23% of each run, Pallas kernels for 0% -> 0%
where the time goes in v1:
time: 1190 us; the launch traced here: 1180 us
  waiting for transfers between devices  772 us (65%)
  matrix products  139 us (12%)
  local copies, waits for them, and re-layouts  126 us (11%)
  other arithmetic  82.6 us (7%)
  blocking collectives  41.2 us (3%)
  between operations  19.6 us (2%)
    reduce_scatter x4, waiting for transfers between devices, per_device(): lax.psum_scatter(partial, 'gx', scatter_dimension=0, tiled=True)  563 us
    all_gather x4, waiting for transfers between devices, per_device(): gathered.append(lax.all_gather(left, 'gy', axis=1, tiled=True))  209 us
    convert_element_type x4, local copies, waits for them, and re-layouts, per_device(): partial = jnp.einsum('kic,kjc->ijc', gathered[b], right, preferred_elemen...  55.6 us
    all_gather x4, local copies, waits for them, and re-layouts, per_device(): gathered.append(lax.all_gather(left, 'gy', axis=1, tiled=True))  52.1 us
    dot_general x8, matrix products, gated(): jnp.einsum('ijc,cd->ijd', normed, part, preferred_element_type=jnp.float32)  51.6 us
    psum x1, blocking collectives, per_device(): mag_total = lax.psum(total, ('gz', 'gx', 'gy'))  41.2 us
    dot_general x4, matrix products, per_device(): jnp.einsum('kic,kjc->ijc', gathered[b], right, preferred_element_type=jnp...  40.6 us
    reduce_sum x5, other arithmetic, layer_norm(): variance = jnp.mean(centered * centered, axis=-1, keepdims=True)  30.3 us
  transfers between devices with their start and end apart: 8, of which 8 were waited for; matrix products, arithmetic and copies ran while one was open for 23% of the time, Pallas kernels for 0%

profile of v1, /device:TPU:0, one launch (start us, length us, event | category | flops | bytes accessed | tf_op | source)
XLA Modules:
  0.0 1181.0 jit_solution(15705465478945079710)
XLA Ops:
  7.2 6.1 convert_reduce_fusion.7
  13.7 12.6 %fusion.38 = (f32[96,96]{1,0:T(8,128)S(1)}, f32[96,96]{1,0:T(8,128)S(1)}, f32[96,96]{1,0:T(8,128)S(1)}, f32[96,96]{1,0:T(8,128)S(1)}) fusion(f32[96,96]{1,0:T(8,128)S(1)} %get-tuple-element.33, bf16[4,96,96,128]{3,2,1,0:T(8,128)(2,1)S(1)} %copy-done.1, f32[96,96]{1,0:T(8,128)S(1)} %get-tuple-element.32, f32[96,96]{1,0:T(8,128)S(1)} %get-tuple-element.30, ...), kind=kLoop, calls=%fused_computation.59 | loop fusion | flops 18837504 | bytes 9732096 | tf_op jit(solution)/shard_map/reduce_sum | solution.py:10
  26.3 5.9 fusion.100
  32.2 6.2 fusion.102
  39.8 9.9 fusion.74
  52.3 6.5 fusion.105
  58.8 6.7 fusion.107
  69.9 6.5 fusion.110
  76.4 6.5 fusion.112
  87.9 6.5 fusion.117
  94.4 6.7 fusion.115
  109.7 39.2 %all-gather.5.cloned.1.call-done = bf16[96,384,128]{2,1,0:T(8,128)(2,1)} async-done(((bf16[96,96,128]{2,1,0:T(8,128)(2,1)}), bf16[96,384,128]{2,1,0:T(8,128)(2,1)}) %all-gather.5.cloned.1.call-update) | async-done | bytes 9437200 | tf_op jit(solution)/shard_map/all_gather | solution.py:37
  148.8 13.0 %copy.63 = bf16[96,384,128]{1,0,2:T(8,128)(2,1)} copy(bf16[96,384,128]{2,1,0:T(8,128)(2,1)} %all-gather.5.cloned.1.call-done) | data formatting | bytes 18874368 | tf_op jit(solution)/shard_map/all_gather | solution.py:37
  161.9 10.2 convert_bitcast_fusion.3
  172.1 13.9 %copy.64 = bf16[384,96,128]{2,1,0:T(8,128)(2,1)} copy(bf16[384,96,128]{0,1,2:T(8,128)(2,1)} %convert_bitcast_fusion.3) | data formatting | bytes 18874368 | tf_op jit(solution)/shard_map/convert_element_type | solution.py:42
  186.1 4.2 copy.69
  190.3 56.6 %all-gather.7.cloned.1.call-done = bf16[96,384,128]{2,1,0:T(8,128)(2,1)} async-done(((bf16[96,96,128]{2,1,0:T(8,128)(2,1)}), bf16[96,384,128]{2,1,0:T(8,128)(2,1)}) %all-gather.7.cloned.1.call-update) | async-done | bytes 9437200 | tf_op jit(solution)/shard_map/all_gather | solution.py:37
  246.9 13.0 %copy.70 = bf16[96,384,128]{1,0,2:T(8,128)(2,1)} copy(bf16[96,384,128]{2,1,0:T(8,128)(2,1)} %all-gather.7.cloned.1.call-done) | data formatting | bytes 18874368 | tf_op jit(solution)/shard_map/all_gather | solution.py:37
  259.9 10.2 convert_bitcast_fusion.2
  270.2 13.9 %copy.71 = bf16[384,96,128]{2,1,0:T(8,128)(2,1)} copy(bf16[384,96,128]{0,1,2:T(8,128)(2,1)} %convert_bitcast_fusion.2) | data formatting | bytes 18874368 | tf_op jit(solution)/shard_map/convert_element_type | solution.py:42
  284.1 4.2 copy.76
  288.3 56.7 %all-gather.9.cloned.1.call-done = bf16[96,384,128]{2,1,0:T(8,128)(2,1)} async-done(((bf16[96,96,128]{2,1,0:T(8,128)(2,1)}), bf16[96,384,128]{2,1,0:T(8,128)(2,1)}) %all-gather.9.cloned.1.call-update) | async-done | bytes 9437200 | tf_op jit(solution)/shard_map/all_gather | solution.py:37
  345.0 13.1 %copy.77 = bf16[96,384,128]{1,0,2:T(8,128)(2,1)} copy(bf16[96,384,128]{2,1,0:T(8,128)(2,1)} %all-gather.9.cloned.1.call-done) | data formatting | bytes 18874368 | tf_op jit(solution)/shard_map/all_gather | solution.py:37
  358.0 10.2 convert_bitcast_fusion.1
  368.2 14.0 %copy.78 = bf16[384,96,128]{2,1,0:T(8,128)(2,1)} copy(bf16[384,96,128]{0,1,2:T(8,128)(2,1)} %convert_bitcast_fusion.1) | data formatting | bytes 18874368 | tf_op jit(solution)/shard_map/convert_element_type | solution.py:42
  382.5 4.2 copy.83
  386.7 56.2 %all-gather.11.cloned.1.call-done = bf16[96,384,128]{2,1,0:T(8,128)(2,1)} async-done(((bf16[96,96,128]{2,1,0:T(8,128)(2,1)}), bf16[96,384,128]{2,1,0:T(8,128)(2,1)}) %all-gather.11.cloned.1.call-update) | async-done | bytes 9437200 | tf_op jit(solution)/shard_map/all_gather | solution.py:37
  442.9 13.0 %copy.84 = bf16[96,384,128]{1,0,2:T(8,128)(2,1)} copy(bf16[96,384,128]{2,1,0:T(8,128)(2,1)} %all-gather.11.cloned.1.call-done) | data formatting | bytes 18874368 | tf_op jit(solution)/shard_map/all_gather | solution.py:37
  455.9 9.9 convert_bitcast_fusion
  465.8 13.8 %copy.85 = bf16[384,96,128]{2,1,0:T(8,128)(2,1)} copy(bf16[384,96,128]{0,1,2:T(8,128)(2,1)} %convert_bitcast_fusion) | data formatting | bytes 18874368 | tf_op jit(solution)/shard_map/convert_element_type | solution.py:42
  479.6 126.7 %reduce-scatter.5.cloned.1.call-done = bf16[96,96,128]{2,1,0:T(8,128)(2,1)} async-done(((bf16[384,96,128]{2,1,0:T(8,128)(2,1)}), bf16[96,96,128]{2,1,0:T(8,128)(2,1)}) %reduce-scatter.5.cloned.1.call-update) | async-done | bytes 2359312 | tf_op jit(solution)/shard_map/reduce_scatter | solution.py:43
  609.0 4.4 fusion.36
  614.0 156.7 %reduce-scatter.7.cloned.1.call-done = bf16[96,96,128]{2,1,0:T(8,128)(2,1)} async-done(((bf16[384,96,128]{2,1,0:T(8,128)(2,1)}), bf16[96,96,128]{2,1,0:T(8,128)(2,1)}) %reduce-scatter.7.cloned.1.call-update) | async-done | bytes 2359312 | tf_op jit(solution)/shard_map/reduce_scatter | solution.py:43
  773.9 4.4 fusion.32
  779.0 156.3 %reduce-scatter.9.cloned.1.call-done = bf16[96,96,128]{2,1,0:T(8,128)(2,1)} async-done(((bf16[384,96,128]{2,1,0:T(8,128)(2,1)}), bf16[96,96,128]{2,1,0:T(8,128)(2,1)}) %reduce-scatter.9.cloned.1.call-update) | async-done | bytes 2359312 | tf_op jit(solution)/shard_map/reduce_scatter | solution.py:43
  937.9 4.5 fusion.28
  942.5 4.2 fusion.84
  946.7 4.2 fusion.86
  951.0 4.2 fusion.88
  955.3 5.8 abs_reduce_fusion.3
  961.1 7.8 abs_reduce_fusion.2
  968.9 8.2 abs_reduce_fusion.1
  977.1 123.2 %reduce-scatter.11.cloned.1.call-done = bf16[96,96,128]{2,1,0:T(8,128)(2,1)} async-done(((bf16[384,96,128]{2,1,0:T(8,128)(2,1)}), bf16[96,96,128]{2,1,0:T(8,128)(2,1)}) %reduce-scatter.11.cloned.1.call-update) | async-done | bytes 2359312 | tf_op jit(solution)/shard_map/reduce_scatter | solution.py:43
  1103.2 4.4 fusion.24
  1107.6 4.2 fusion.90
  1111.8 8.2 abs_reduce_fusion
  1122.5 41.2 %psum.7 = f32[]{:T(128)} all-reduce(f32[]{:T(128)S(6)} %add.203), channel_id=1, replica_groups=mesh['gz'=2,'gx'=4,'gy'=4] {'gz','gx','gy'}, use_global_device_ids=true, to_apply=%region_24.0 | all-reduce | flops 1 | bytes 8 | tf_op jit(solution)/shard_map/psum | solution.py:61
  1164.3 8.2 pad_maximum_fusion
  (125 shorter events, 34.9 us)
Async XLA Ops:
  7.2 935.3 %copy-start = (bf16[128,128]{1,0:T(8,128)(2,1)S(1)}, bf16[128,128]{1,0:T(8,128)(2,1)}, u32[]{:S(2)}) copy-start(bf16[128,128]{1,0:T(8,128)(2,1)} %param.7) | copy-start | bytes 98308
  7.2 141.6 %all-gather.5.cloned.1.call-start = ((), (), s32[]{:S(2)}) async-start(), calls=%async_computation.4 | async-start | bytes 11796480 | tf_op jit(solution)/shard_map/all_gather | solution.py:37
  7.2 6.5 copy-start.1
  13.4 18.8 %copy-start.10 = (f32[96,96]{1,0:T(8,128)}, f32[96,96]{1,0:T(8,128)S(1)}, u32[]{:S(2)}) copy-start(f32[96,96]{1,0:T(8,128)S(1)} %get-tuple-element.33) | copy-start | bytes 110596
  13.4 45.4 %copy-start.8 = (f32[96,96]{1,0:T(8,128)}, f32[96,96]{1,0:T(8,128)S(1)}, u32[]{:S(2)}) copy-start(f32[96,96]{1,0:T(8,128)S(1)} %get-tuple-element.32) | copy-start | bytes 110596
  13.7 12.6 %copy-start.6 = (bf16[128,640]{1,0:T(8,128)(2,1)S(1)}, bf16[128,640]{1,0:T(8,128)(2,1)}, u32[]{:S(2)}) copy-start(bf16[128,640]{1,0:T(8,128)(2,1)} %param.6) | copy-start | bytes 491524
  26.3 5.9 copy-start.12
  32.2 6.2 copy-start.34
  39.8 9.9 copy-start.24
  49.7 197.2 %all-gather.7.cloned.1.call-start = ((), (), s32[]{:S(2)}) async-start(), calls=%async_computation.6 | async-start | bytes 11796480 | tf_op jit(solution)/shard_map/all_gather | solution.py:37
  52.2 13.3 %copy-start.26 = (f32[96,96]{1,0:T(8,128)}, f32[96,96]{1,0:T(8,128)S(1)}, u32[]{:S(2)}) copy-start(f32[96,96]{1,0:T(8,128)S(1)} %broadcast_multiply_fusion.2) | copy-start | bytes 110596
  52.3 6.6 copy-start.14
  69.7 275.2 %all-gather.9.cloned.1.call-start = ((), (), s32[]{:S(2)}) async-start(), calls=%async_computation.8 | async-start | bytes 11796480 | tf_op jit(solution)/shard_map/all_gather | solution.py:37
  69.9 13.1 %copy-start.28 = (f32[96,96]{1,0:T(8,128)}, f32[96,96]{1,0:T(8,128)S(1)}, u32[]{:S(2)}) copy-start(f32[96,96]{1,0:T(8,128)S(1)} %broadcast_multiply_fusion.1) | copy-start | bytes 110596
  69.9 6.5 copy-start.16
  87.1 355.8 %all-gather.11.cloned.1.call-start = ((), (), s32[]{:S(2)}) async-start(), calls=%async_computation.10 | async-start | bytes 11796480 | tf_op jit(solution)/shard_map/all_gather | solution.py:37
  87.8 13.3 %copy-start.30 = (f32[96,96]{1,0:T(8,128)}, f32[96,96]{1,0:T(8,128)S(1)}, u32[]{:S(2)}) copy-start(f32[96,96]{1,0:T(8,128)S(1)} %broadcast_multiply_fusion) | copy-start | bytes 110596
  87.9 6.5 copy-start.18
  105.2 501.1 %reduce-scatter.5.cloned.1.call-start = ((), (), s32[]{:S(2)}) async-start(), calls=%async_computation.5 | async-start | bytes 11796480 | tf_op jit(solution)/shard_map/reduce_scatter | solution.py:43
  186.1 584.7 %reduce-scatter.7.cloned.1.call-start = ((), (), s32[]{:S(2)}) async-start(), calls=%async_computation.7 | async-start | bytes 11796480 | tf_op jit(solution)/shard_map/reduce_scatter | solution.py:43
  284.1 651.2 %reduce-scatter.9.cloned.1.call-start = ((), (), s32[]{:S(2)}) async-start(), calls=%async_computation.9 | async-start | bytes 11796480 | tf_op jit(solution)/shard_map/reduce_scatter | solution.py:43
  382.3 718.1 %reduce-scatter.11.cloned.1.call-start = ((), (), s32[]{:S(2)}) async-start(), calls=%async_computation.11 | async-start | bytes 11796480 | tf_op jit(solution)/shard_map/reduce_scatter | solution.py:43
  609.0 4.4 copy-start.20
  614.0 328.5 %copy-start.2 = (bf16[96,96,128]{2,1,0:T(8,128)(2,1)S(1)}, bf16[96,96,128]{2,1,0:T(8,128)(2,1)}, u32[]{:S(2)}) copy-start(bf16[96,96,128]{2,1,0:T(8,128)(2,1)} %reduce-scatter.5.cloned.1.call-done) | copy-start | bytes 7077892
  773.3 0.6 copy-start.22
  773.9 181.3 %slice-start = ((s8[9437184]{0:T(1024)(128)(4,1)}), s8[1048576]{0:T(1024)(128)(4,1)S(1)}, s32[]{:S(2)}) async-start(s8[9437184]{0:T(1024)(128)(4,1)} %bitcast.152), calls=%async_computation.12 | async-start | bytes 2097152
  935.3 7.2 copy-start.21
  935.3 7.2 copy-start.32
  937.9 8.8 copy-start.3
  937.9 8.8 copy-start.23
  937.9 8.8 copy-start.33
  942.5 12.7 %slice-start.1 = ((s8[9437184]{0:T(1024)(128)(4,1)}), s8[4194304]{0:T(1024)(128)(4,1)S(1)}, s32[]{:S(2)}) async-start(s8[9437184]{0:T(1024)(128)(4,1)} %bitcast.152), calls=%async_computation.13 | async-start | bytes 8388608
  946.7 4.2 copy-start.5
  946.7 8.5 slice-start.2
  951.0 4.3 copy-start.7
  951.0 4.3 copy-start.11
  951.0 4.3 copy-start.13
  951.0 4.3 copy-start.25
  955.3 5.8 copy-start.9
  955.3 5.8 copy-start.15
  955.3 5.8 copy-start.27
  961.1 7.8 copy-start.17
  961.1 7.8 copy-start.29
  1100.4 7.2 copy-start.4
  1103.1 8.6 copy-start.19
  1103.1 8.6 copy-start.31
Sparse Core Ops, SparseCore 0:
  49.8 98.9 all-gather.4
  150.7 96.1 all-gather.6
  248.7 96.1 all-gather.8
  346.7 96.1 all-gather.10
  445.1 161.1 reduce-scatter.4
  608.6 162.1 reduce-scatter.6
  773.1 162.1 reduce-scatter.8
  938.2 162.1 reduce-scatter.10
